TPU v7x, 32 devices: a whole 2x2x4 slice. The times are simulated.
32 devices in a mesh: pole: 2 (over x), row: 8 (over z, y), col: 2 (over core).
Axes of the slice: x: 2, y: 2, z: 4, core: 2. Of those that a mesh axis runs over, the one named last changes fastest.
Arguments:
- ancestor_inverse: float32 [2, 24576, 12288], P(None, ('pole', 'row'), 'col'), parts along dimension 1, may hold values from -6 to 6
- factor_panels: float32 [4, 2, 24576, 128], P(None, None, ('pole', 'col', 'row')), parts along dimension 2, may hold values from -0.0546875 to 0.0546875
- diag_inverse: float32 [8, 2, 128, 128], P('pole'), parts along dimension 0, may hold values from -6 to 6
- coupling: float32 [4, 2, 128, 128], P('pole'), parts along dimension 0, may hold values from -0.5 to 0.5
- block_pattern: int32 [4, 96], replicated, may hold values from 0 to 1, as said below
- tree_order: int32 [4], replicated, may hold values from 0 to 3, each once
Outputs:
- inverse_panels: float32 [4, 2, 24576, 128], P(None, None, ('pole', 'row')), parts along dimension 2
- inverse_diagonal: float32 [8, 2, 128, 128], P('pole'), parts along dimension 0
- inverse_coupling: float32 [4, 2, 128, 128], P('pole'), parts along dimension 0
There are 2 independent parts, one for each index of `pole`. A program takes and returns all parts, laid end to end along the dimension named above; an argument that names none is the same for every part. Nothing has to cross between parts.
Inputs may be any that keep to these rules, and one draw needn't show every extreme that they name: `tree_order`: each supernode number appears once. `block_pattern`: blocks 0 and 48 lie in every supernode's structure.
All inputs are finite; a program needn't handle non-finite values.
Results may differ from a plain program's by a relative error of at most 0.0001.
Values sent between devices are 32-bit elements; how exact they have to be, the bound alone decides.
A program may use at most 192 MiB of HBM per device.

v0:
```python
import jax
import jax.numpy as jnp
from jax import lax
from jax.sharding import PartitionSpec as P


def swapped(block, axis, bit):
    count = lax.axis_size(axis)
    route = []
    for low in range(count):
        high = low | 1 << bit
        if high != low and high < count:
            route += [(low, high), (high, low)]
    return lax.ppermute(block, axis, route)


def matmul(left_side, right_side):
    return jnp.dot(
        left_side, right_side, preferred_element_type=jnp.float32, precision=lax.Precision.HIGHEST
    )


def multiply(left_side, right_side):
    real_part = matmul(left_side[0], right_side[0]) - matmul(left_side[1], right_side[1])
    imag_part = matmul(left_side[0], right_side[1]) + matmul(left_side[1], right_side[0])
    return jnp.stack([real_part, imag_part])


def flipped(matrix):
    return jnp.swapaxes(matrix, 1, 2)


def row_masks(pattern_eff, first_row, row_count, block_rows):
    row_index = first_row + jnp.arange(row_count, dtype=jnp.int32)
    blocks = row_index // block_rows
    onehot = (blocks[:, None] == jnp.arange(pattern_eff.shape[1], dtype=jnp.int32)[None, :]).astype(
        jnp.float32
    )
    return matmul(pattern_eff, onehot.T)


def per_device(ancestor_inverse, factor_panels, diag_inverse, coupling, block_pattern, tree_order):
    grid_row = lax.axis_index("row")
    grid_col = lax.axis_index("col")
    tile_rows = ancestor_inverse.shape[1]
    half_rows = ancestor_inverse.shape[2]
    piece_rows = factor_panels.shape[2]
    block_rows = factor_panels.shape[3]
    super_count = factor_panels.shape[0]
    share_rows = tile_rows // 2
    sorted_pattern = jnp.take(block_pattern, tree_order, axis=0).astype(jnp.float32)
    pattern_eff = jnp.concatenate(
        [sorted_pattern[:2], sorted_pattern[2:] * sorted_pattern[:2]], axis=0
    )
    source_mask = row_masks(
        pattern_eff, grid_col * half_rows + grid_row * piece_rows, piece_rows, block_rows
    )
    target_mask = row_masks(pattern_eff, grid_row * tile_rows, tile_rows, block_rows)
    panels = jnp.take(factor_panels, tree_order, axis=0) * source_mask[:, None, :, None]
    diag_blocks = jnp.take(diag_inverse, tree_order, axis=0)
    columns = []
    products = []
    for tree_slot in range(super_count):
        gathered = lax.all_gather(panels[tree_slot], "row", axis=1, tiled=True)
        columns.append(gathered)
        products.append(lax.psum(multiply(ancestor_inverse, gathered), "col"))
    own_flag = (grid_row * tile_rows // half_rows == grid_col).astype(jnp.float32)
    offset = jnp.clip(grid_row * tile_rows - grid_col * half_rows, 0, half_rows - tile_rows)
    own_windows = jnp.stack(
        [
            lax.dynamic_slice_in_dim(column_set, offset, tile_rows, 1) * own_flag
            for column_set in columns
        ]
    )
    partner_windows = swapped(own_windows, "col", 0)
    tile_windows = own_windows + partner_windows

    def share(matrix):
        return lax.dynamic_slice_in_dim(matrix, grid_col * share_rows, share_rows, 1)

    windows = [share(tile_windows[tree_slot]) for tree_slot in range(super_count)]
    parent_cols = [
        -target_mask[tree_slot][None, :, None] * products[tree_slot] for tree_slot in range(2)
    ]
    child_cols = [
        -target_mask[tree_slot + 2][None, :, None]
        * (products[tree_slot + 2] + multiply(parent_cols[tree_slot], coupling[tree_slot]))
        for tree_slot in range(2)
    ]
    parent_local = [
        multiply(flipped(windows[tree_slot]), share(parent_cols[tree_slot]))
        for tree_slot in range(2)
    ]
    cross_local = [
        multiply(flipped(share(parent_cols[tree_slot])), windows[tree_slot + 2])
        for tree_slot in range(2)
    ]
    child_local = [
        multiply(flipped(windows[tree_slot + 2]), share(child_cols[tree_slot]))
        for tree_slot in range(2)
    ]
    parent_sums = lax.psum(jnp.stack(parent_local), ("row", "col"))
    parent_diag = [diag_blocks[tree_slot] - parent_sums[tree_slot] for tree_slot in range(2)]
    child_totals = lax.psum(jnp.stack(cross_local + child_local), ("row", "col"))
    crosses = [
        -(child_totals[tree_slot] + multiply(parent_diag[tree_slot], coupling[tree_slot]))
        for tree_slot in range(2)
    ]
    child_sums = [child_totals[2 + tree_slot] for tree_slot in range(2)]
    child_diag = [
        diag_blocks[tree_slot + 2]
        - child_sums[tree_slot]
        - multiply(flipped(coupling[tree_slot]), crosses[tree_slot])
        for tree_slot in range(2)
    ]
    all_cols = jnp.stack(parent_cols + child_cols)
    all_diag = jnp.stack(parent_diag + child_diag)
    inverse_panels = jnp.zeros_like(all_cols).at[tree_order].set(all_cols)
    inverse_diagonal = jnp.zeros_like(all_diag).at[tree_order].set(all_diag)
    return (inverse_panels, inverse_diagonal, jnp.stack(crosses))


def solution(mesh):
    return jax.shard_map(
        per_device,
        mesh=mesh,
        in_specs=(
            P(None, ("pole", "row"), "col"),
            P(None, None, ("pole", "col", "row"), None),
            P("pole", None, None, None),
            P("pole", None, None, None),
            P(),
            P(),
        ),
        out_specs=(
            P(None, None, ("pole", "row"), None),
            P("pole", None, None, None),
            P("pole", None, None, None),
        ),
        check_vma=False,
    )
```

profile of v0, /device:TPU:0, one launch (start us, length us, event | category | flops | bytes accessed | tf_op | source)
XLA Modules:
  0.0 873.5 jit_solution(7536772676169645142)
XLA Ops:
  7.2 0.8 compare_and_fusion
  9.3 1.2 gather_fusion
  10.7 2.4 gather_fusion.1
  13.5 2.4 select_multiply_fusion
  15.8 1.7 fusion.222
  19.7 99.5 %all-gather.11.cloned.1.call-done = f32[1,2,6144,128]{3,2,1,0:T(8,128)} async-done(((f32[1,2,768,128]{3,2,1,0:T(8,128)}), f32[1,2,6144,128]{3,2,1,0:T(8,128)}) %all-gather.11.cloned.1.call-update) | async-done | bytes 6291472 | tf_op jit(solution)/shard_map/all_gather | solution.py:64
  119.2 36.1 %fusion.8 = f32[128,1536]{1,0:T(8,128)S(1)} fusion(f32[2,1536,6144]{2,1,0:T(8,128)} %param.6, f32[1,2,6144,128]{3,2,1,0:T(8,128)} %all-gather.11.cloned.1.call-done), kind=kOutput, calls=%fused_computation.13 | convolution fusion | flops 14495514624 | bytes 41680896 | tf_op jit(solution)/shard_map/dot_general | solution.py:18
  155.3 35.0 %fusion.10 = f32[128,1536]{1,0:T(8,128)S(1)} fusion(f32[2,1536,6144]{2,1,0:T(8,128)} %param.6, f32[1,2,6144,128]{3,2,1,0:T(8,128)S(1)} %copy-done.2), kind=kOutput, calls=%fused_computation.15 | convolution fusion | flops 14495514624 | bytes 41680896 | tf_op jit(solution)/shard_map/dot_general | solution.py:18
  190.3 35.3 %fusion.73 = f32[1,1536,128]{1,2,0:T(8,128)S(1)} fusion(f32[128,1536]{1,0:T(8,128)S(1)} %fusion.8, f32[2,1536,6144]{2,1,0:T(8,128)} %param.6, f32[1,2,6144,128]{3,2,1,0:T(8,128)S(1)} %copy-done.2), kind=kOutput, calls=%fused_computation.79 | convolution fusion | flops 14495711232 | bytes 42467328 | tf_op jit(solution)/shard_map/dot_general | solution.py:18
  225.6 35.6 %fusion.67 = f32[1,1536,128]{1,2,0:T(8,128)S(1)} fusion(f32[128,1536]{1,0:T(8,128)S(1)} %fusion.10, f32[2,1536,6144]{2,1,0:T(8,128)} %param.6, f32[1,2,6144,128]{3,2,1,0:T(8,128)S(1)} %copy-done.2), kind=kOutput, calls=%fused_computation.77 | convolution fusion | flops 14495711232 | bytes 42467328 | tf_op jit(solution)/shard_map/dot_general | solution.py:18
  261.3 36.6 %fusion.4 = f32[128,1536]{1,0:T(8,128)S(1)} fusion(f32[2,1536,6144]{2,1,0:T(8,128)} %param.6, f32[1,2,6144,128]{3,2,1,0:T(8,128)} %all-gather.13.cloned.1.call-done), kind=kOutput, calls=%fused_computation.9 | convolution fusion | flops 14495514624 | bytes 41680896 | tf_op jit(solution)/shard_map/dot_general | solution.py:18
  297.9 35.2 %fusion.6 = f32[128,1536]{1,0:T(8,128)S(1)} fusion(f32[2,1536,6144]{2,1,0:T(8,128)} %param.6, f32[1,2,6144,128]{3,2,1,0:T(8,128)S(1)} %copy-done.3), kind=kOutput, calls=%fused_computation.11 | convolution fusion | flops 14495514624 | bytes 41680896 | tf_op jit(solution)/shard_map/dot_general | solution.py:18
  333.0 1.3 pad_maximum_fusion.3
  334.4 35.2 %fusion.85 = f32[1,1536,128]{1,2,0:T(8,128)S(1)} fusion(f32[128,1536]{1,0:T(8,128)S(1)} %fusion.4, f32[2,1536,6144]{2,1,0:T(8,128)} %param.6, f32[1,2,6144,128]{3,2,1,0:T(8,128)S(1)} %copy-done.3), kind=kOutput, calls=%fused_computation.83 | convolution fusion | flops 14495711232 | bytes 42467328 | tf_op jit(solution)/shard_map/dot_general | solution.py:18
  369.6 35.0 %fusion.79 = f32[1,1536,128]{1,2,0:T(8,128)S(1)} fusion(f32[128,1536]{1,0:T(8,128)S(1)} %fusion.6, f32[2,1536,6144]{2,1,0:T(8,128)} %param.6, f32[1,2,6144,128]{3,2,1,0:T(8,128)S(1)} %copy-done.3), kind=kOutput, calls=%fused_computation.81 | convolution fusion | flops 14495711232 | bytes 42467328 | tf_op jit(solution)/shard_map/dot_general | solution.py:18
  404.7 1.3 pad_maximum_fusion.4
  405.9 36.3 %fusion = f32[128,1536]{1,0:T(8,128)S(1)} fusion(f32[2,1536,6144]{2,1,0:T(8,128)} %param.6, f32[1,2,6144,128]{3,2,1,0:T(8,128)} %all-gather.15.cloned.1.call-done), kind=kOutput, calls=%fused_computation.5 | convolution fusion | flops 14495514624 | bytes 41680896 | tf_op jit(solution)/shard_map/dot_general | solution.py:18
  442.3 35.0 %fusion.2 = f32[128,1536]{1,0:T(8,128)S(1)} fusion(f32[2,1536,6144]{2,1,0:T(8,128)} %param.6, f32[1,2,6144,128]{3,2,1,0:T(8,128)S(1)} %copy-done.4), kind=kOutput, calls=%fused_computation.7 | convolution fusion | flops 14495514624 | bytes 41680896 | tf_op jit(solution)/shard_map/dot_general | solution.py:18
  477.3 35.5 %fusion.97 = f32[1,1536,128]{1,2,0:T(8,128)S(1)} fusion(f32[128,1536]{1,0:T(8,128)S(1)} %fusion, f32[2,1536,6144]{2,1,0:T(8,128)} %param.6, f32[1,2,6144,128]{3,2,1,0:T(8,128)S(1)} %copy-done.4), kind=kOutput, calls=%fused_computation.87 | convolution fusion | flops 14495711232 | bytes 42467328 | tf_op jit(solution)/shard_map/dot_general | solution.py:18
  512.8 35.0 %fusion.91 = f32[1,1536,128]{1,2,0:T(8,128)S(1)} fusion(f32[128,1536]{1,0:T(8,128)S(1)} %fusion.2, f32[2,1536,6144]{2,1,0:T(8,128)} %param.6, f32[1,2,6144,128]{3,2,1,0:T(8,128)S(1)} %copy-done.4), kind=kOutput, calls=%fused_computation.85 | convolution fusion | flops 14495711232 | bytes 42467328 | tf_op jit(solution)/shard_map/dot_general | solution.py:18
  547.9 1.2 pad_maximum_fusion.5
  549.1 36.3 %fusion.12 = f32[128,1536]{1,0:T(8,128)S(1)} fusion(f32[2,1536,6144]{2,1,0:T(8,128)} %param.6, f32[1,2,6144,128]{3,2,1,0:T(8,128)} %all-gather.9.cloned.1.call-done), kind=kOutput, calls=%fused_computation.17 | convolution fusion | flops 14495514624 | bytes 41680896 | tf_op jit(solution)/shard_map/dot_general | solution.py:18
  585.4 35.0 %fusion.14 = f32[128,1536]{1,0:T(8,128)S(1)} fusion(f32[2,1536,6144]{2,1,0:T(8,128)} %param.6, f32[1,2,6144,128]{3,2,1,0:T(8,128)S(1)} %copy-done.5), kind=kOutput, calls=%fused_computation.19 | convolution fusion | flops 14495514624 | bytes 41680896 | tf_op jit(solution)/shard_map/dot_general | solution.py:18
  620.5 35.5 %fusion.61 = f32[1,1536,128]{1,2,0:T(8,128)S(1)} fusion(f32[128,1536]{1,0:T(8,128)S(1)} %fusion.12, f32[2,1536,6144]{2,1,0:T(8,128)} %param.6, f32[1,2,6144,128]{3,2,1,0:T(8,128)S(1)} %copy-done.5), kind=kOutput, calls=%fused_computation.75 | convolution fusion | flops 14495711232 | bytes 42467328 | tf_op jit(solution)/shard_map/dot_general | solution.py:18
  655.9 35.0 %fusion.55 = f32[1,1536,128]{1,2,0:T(8,128)S(1)} fusion(f32[128,1536]{1,0:T(8,128)S(1)} %fusion.14, f32[2,1536,6144]{2,1,0:T(8,128)} %param.6, f32[1,2,6144,128]{3,2,1,0:T(8,128)S(1)} %copy-done.5), kind=kOutput, calls=%fused_computation.73 | convolution fusion | flops 14495711232 | bytes 42467328 | tf_op jit(solution)/shard_map/dot_general | solution.py:18
  691.0 1.3 pad_maximum_fusion.2
  692.4 1.6 dynamic-slice_multiply_fusion.2
  694.0 2.2 dynamic-slice_multiply_fusion.1
  696.2 2.3 dynamic-slice_multiply_fusion
  698.5 2.5 dynamic-slice_multiply_fusion.3
  701.1 2.9 pad_maximum_fusion.1
  704.5 1.7 gather_fusion.2
  708.2 1.5 broadcast_select_fusion
  709.7 13.4 %all-reduce.7.cloned.1.call-done = (f32[2,1536,128]{1,2,0:T(8,128)}, f32[2,1536,128]{1,2,0:T(8,128)}, f32[2,1536,128]{1,2,0:T(8,128)}, f32[2,1536,128]{1,2,0:T(8,128)}) async-done(((f32[2,1536,128]{1,2,0:T(8,128)}, f32[2,1536,128]{1,2,0:T(8,128)}, f32[2,1536,128]{1,2,0:T(8,128)}, f32[2,1536,128]{1,2,0:T(8,128)}), (f32[2,1536,128]{1,2,0:T(8,128)}, f32[2,1536,128]{1,2,0:T(8,128)}, f32[2,1536,128]{1,2,0:T(8,128)}, ...) | async-done | bytes 6291472 | tf_op jit(solution)/shard_map/psum | solution.py:66
  723.1 1.7 broadcast_multiply_fusion
  725.3 0.8 fusion.121
  726.2 0.8 fusion.122
  727.0 0.8 fusion.119
  727.9 0.8 fusion.120
  728.8 1.4 fusion.225
  730.2 1.4 fusion.224
  732.7 3.3 fusion.220
  737.4 0.8 fusion.127
  738.2 0.8 fusion.125
  740.9 0.9 fusion.51
  741.8 0.9 fusion.50
  742.7 0.9 fusion.49
  743.7 0.9 fusion.48
  746.2 0.8 fusion.135
  751.4 0.8 fusion.115
  753.0 0.8 fusion.117
  755.7 0.8 fusion.107
  757.3 0.8 fusion.109
  760.0 0.8 pad_maximum_fusion.6
  760.9 4.3 pad_maximum_fusion
  765.2 6.6 copy.33
  771.8 3.2 broadcast_in_dim.45
  775.0 13.3 %scatter_fusion = f32[4,2,1536,128]{3,2,1,0:T(8,128)} fusion(f32[4,2,1536,128]{3,2,1,0:T(8,128)} %broadcast_in_dim.45, s32[4]{0:T(128)S(1)} %copy-done.32, f32[4,2,1536,128]{3,2,1,0:T(8,128)} %copy.33), kind=kCustom, calls=%fused_computation.3 | custom fusion | bytes 18874384 | tf_op jit(solution)/shard_map/scatter | solution.py:118
  788.3 66.6 %all-reduce.5.cloned.1.call-done = (f32[4,2,128,128]{3,2,1,0:T(8,128)}, f32[2,2,128,128]{3,2,1,0:T(8,128)}) async-done(((f32[4,2,128,128]{3,2,1,0:T(8,128)}, f32[2,2,128,128]{3,2,1,0:T(8,128)}), (f32[4,2,128,128]{3,2,1,0:T(8,128)}, f32[2,2,128,128]{3,2,1,0:T(8,128)})) %all-reduce.5.cloned.1.call-update) | async-done | bytes 786448 | tf_op jit(solution)/shard_map/psum | solution.py:104
  854.9 1.1 slice_subtract_fusion.3
  857.7 1.0 fusion.140
  861.9 0.8 pad_maximum_fusion.7
  862.7 0.8 broadcast_in_dim.51
  863.6 2.7 scatter_fusion.1
  (151 shorter events, 27.0 us)
Async XLA Ops:
  7.2 3.5 copy-start
  7.2 112.0 %all-gather.11.cloned.1.call-start = ((), (), s32[]{:S(2)}) async-start(), calls=%async_computation.1 | async-start | bytes 7077888 | tf_op jit(solution)/shard_map/all_gather | solution.py:64
  8.0 5.4 copy-start.33
  8.8 0.5 copy-start.31
  9.3 3.8 copy-start.30
  10.6 2.4 copy-start.34
  10.6 2.4 copy-start.36
  17.6 243.7 %all-gather.13.cloned.1.call-start = ((), (), s32[]{:S(2)}) async-start(), calls=%async_computation.2 | async-start | bytes 7077888 | tf_op jit(solution)/shard_map/all_gather | solution.py:64
  18.3 387.6 %all-gather.15.cloned.1.call-start = ((), (), s32[]{:S(2)}) async-start(), calls=%async_computation.3 | async-start | bytes 7077888 | tf_op jit(solution)/shard_map/all_gather | solution.py:64
  19.1 530.0 %all-gather.9.cloned.1.call-start = ((), (), s32[]{:S(2)}) async-start(), calls=%async_computation | async-start | bytes 7077888 | tf_op jit(solution)/shard_map/all_gather | solution.py:64
  19.7 703.5 %all-reduce.7.cloned.1.call-start = ((), (), s32[]{:S(2)}) async-start(), calls=%async_computation.5 | async-start | bytes 12582912 | tf_op jit(solution)/shard_map/psum | solution.py:66
  119.2 36.1 %copy-start.2 = (f32[1,2,6144,128]{3,2,1,0:T(8,128)S(1)}, f32[1,2,6144,128]{3,2,1,0:T(8,128)}, u32[]{:S(2)}) copy-start(f32[1,2,6144,128]{3,2,1,0:T(8,128)} %all-gather.11.cloned.1.call-done) | copy-start | bytes 18874372
  261.3 36.6 %copy-start.3 = (f32[1,2,6144,128]{3,2,1,0:T(8,128)S(1)}, f32[1,2,6144,128]{3,2,1,0:T(8,128)}, u32[]{:S(2)}) copy-start(f32[1,2,6144,128]{3,2,1,0:T(8,128)} %all-gather.13.cloned.1.call-done) | copy-start | bytes 18874372
  405.9 36.3 %copy-start.4 = (f32[1,2,6144,128]{3,2,1,0:T(8,128)S(1)}, f32[1,2,6144,128]{3,2,1,0:T(8,128)}, u32[]{:S(2)}) copy-start(f32[1,2,6144,128]{3,2,1,0:T(8,128)} %all-gather.15.cloned.1.call-done) | copy-start | bytes 18874372
  549.1 36.3 %copy-start.5 = (f32[1,2,6144,128]{3,2,1,0:T(8,128)S(1)}, f32[1,2,6144,128]{3,2,1,0:T(8,128)}, u32[]{:S(2)}) copy-start(f32[1,2,6144,128]{3,2,1,0:T(8,128)} %all-gather.9.cloned.1.call-done) | copy-start | bytes 18874372
  692.3 162.6 %all-reduce.5.cloned.1.call-start = ((), (), s32[]{:S(2)}) async-start(), calls=%async_computation.4 | async-start | bytes 1572864 | tf_op jit(solution)/shard_map/psum | solution.py:104
  694.0 7.1 copy-start.10
  696.2 4.9 copy-start.12
  698.5 5.5 copy-start.14
  701.1 3.4 copy-start.16
  701.1 5.2 copy-start.35
  701.1 5.2 copy-start.37
  701.1 6.4 copy-start.18
  704.5 27.2 %collective-permute-start = (f32[4,2,1536,128]{3,2,1,0:T(8,128)}, f32[4,2,1536,128]{3,2,1,0:T(8,128)}, u32[]{:S(2)}, u32[]{:S(2)}) collective-permute-start(f32[4,2,1536,128]{3,2,1,0:T(8,128)} %pad_maximum_fusion.1), channel_id=1, source_target_pairs={{0,1},{1,0},{2,3},{3,2},{4,5},{5,4},{6,7},{7,6},{8,9},{9,8},{10,11... | collective-permute-start | bytes 18874376 | tf_op jit(solution)/shard_map/ppermute | solution.py:14
  723.1 1.9 copy-start.19
  725.3 3.4 copy-start.20
  728.8 2.9 copy-start.11
  728.8 2.9 copy-start.13
  728.8 3.5 copy-start.15
  728.8 3.9 copy-start.17
  743.6 1.4 copy-start.23
  743.6 1.9 copy-start.24
  743.6 1.9 copy-start.28
  743.7 1.9 copy-start.29
  746.2 9.5 %copy-start.8 = (f32[2,1536,128]{1,2,0:T(8,128)}, f32[2,1536,128]{1,2,0:T(8,128)S(1)}, u32[]{:S(2)}) copy-start(f32[2,1536,128]{1,2,0:T(8,128)S(1)} %get-tuple-element.36) | copy-start | bytes 4718596
  746.2 11.1 %copy-start.6 = (f32[2,1536,128]{1,2,0:T(8,128)}, f32[2,1536,128]{1,2,0:T(8,128)S(1)}, u32[]{:S(2)}) copy-start(f32[2,1536,128]{1,2,0:T(8,128)S(1)} %get-tuple-element.35) | copy-start | bytes 4718596
  757.3 3.5 copy-start.9
  758.1 2.7 copy-start.7
  771.8 3.2 copy-start.32
  775.0 79.9 %copy-start.21 = (f32[4,2,128,128]{3,2,1,0:T(8,128)S(1)}, f32[4,2,128,128]{3,2,1,0:T(8,128)}, u32[]{:S(2)}) copy-start(f32[4,2,128,128]{3,2,1,0:T(8,128)} %broadcast_select_fusion) | copy-start | bytes 1572868
  788.3 70.4 %copy-start.26 = (f32[2,128,128]{1,2,0:T(8,128)S(1)}, f32[2,128,128]{1,2,0:T(8,128)}, u32[]{:S(2)}) copy-start(f32[2,128,128]{1,2,0:T(8,128)} %get-tuple-element.31) | copy-start | bytes 393220
  854.9 5.0 copy-start.27
  854.9 6.2 copy-start.22
  854.9 6.2 copy-start.25
  859.9 6.4 copy-start.1
Sparse Core Ops, SparseCore 0:
  17.7 101.4 all-gather.10
  121.4 96.8 all-gather.12
  220.5 96.9 all-gather.14
  320.1 96.8 all-gather.8
  692.4 30.6 all-reduce.6
  761.0 93.8 all-reduce.4
where the time goes:
time: 883 us; the launch traced here: 874 us
  matrix products  597 us (68%)
  waiting for transfers between devices  181 us (20%)
  other arithmetic  41.3 us (5%)
  local copies, waits for them, and re-layouts  38.3 us (4%)
  between operations  15.6 us (2%)
    dot_general x66, matrix products, matmul(): jnp.dot(left_side, right_side, preferred_element_type=jnp.float32, precis...  597 us
    all_gather x4, waiting for transfers between devices, per_device(): gathered = lax.all_gather(panels[tree_slot], 'row', axis=1, tiled=True)  99.5 us
    psum x1, waiting for transfers between devices, per_device(): lax.psum(jnp.stack(cross_local + child_local), ('row', 'col'))  66.6 us
  transfers between devices with their start and end apart: 7, of which 3 were waited for; matrix products, arithmetic and copies ran while one was open for 55% of the time, Pallas kernels for 0%

commit v1 on v0

--- a/solution.py
+++ b/solution.py
@@ -1,7 +1,17 @@
+import functools
 import jax
 import jax.numpy as jnp
 from jax import lax
 from jax.sharding import PartitionSpec as P
+
+
+def return_all_notes(unit, row_axis, axis_key):
+    for w in (row_axis, axis_key):
+        unit = lax.psum(unit, w)
+    return unit
+
+
+step_on_ticks_now = functools.partial(return_all_notes, row_axis="col", axis_key="row")
 
 
 def swapped(block, axis, bit):
@@ -101,7 +111,7 @@
     ]
     parent_sums = lax.psum(jnp.stack(parent_local), ("row", "col"))
     parent_diag = [diag_blocks[tree_slot] - parent_sums[tree_slot] for tree_slot in range(2)]
-    child_totals = lax.psum(jnp.stack(cross_local + child_local), ("row", "col"))
+    child_totals = step_on_ticks_now(jnp.stack(cross_local + child_local))
     crosses = [
         -(child_totals[tree_slot] + multiply(parent_diag[tree_slot], coupling[tree_slot]))
         for tree_slot in range(2)

time: 883 us -> 978 us (1.11)
  waiting for transfers between devices: 181 us -> 264 us
  matrix products: 597 us -> 610 us
    psum x1 -> x3, waiting for transfers between devices: 66.6 us -> 148 us  [the longest x2 96 us: return_all_notes(): unit = lax.psum(unit, w)]
    dot_general x66, matrix products: 597 us -> 610 us  [matmul(): jnp.dot(left_side, right_side, preferred_element_type=jnp.float32, precis...]
  transfers between devices with their start and end apart: 7 -> 9, of which waited for: 3 -> 5; matrix products, arithmetic and copies ran while one was open for 55% -> 51% of each run, Pallas kernels for 0% -> 0%
where the time goes in v1:
time: 978 us; the launch traced here: 969 us
  matrix products  610 us (62%)
  waiting for transfers between devices  264 us (27%)
  other arithmetic  41 us (4%)
  local copies, waits for them, and re-layouts  38.2 us (4%)
  between operations  15.8 us (2%)
    dot_general x66, matrix products, matmul(): jnp.dot(left_side, right_side, preferred_element_type=jnp.float32, precis...  610 us
    all_gather x4, waiting for transfers between devices, per_device(): gathered = lax.all_gather(panels[tree_slot], 'row', axis=1, tiled=True)  99.5 us
    psum x2, waiting for transfers between devices, return_all_notes(): unit = lax.psum(unit, w)  96 us
    psum x1, waiting for transfers between devices, per_device(): parent_sums = lax.psum(jnp.stack(parent_local), ('row', 'col'))  51.7 us
  transfers between devices with their start and end apart: 9, of which 5 were waited for; matrix products, arithmetic and copies ran while one was open for 51% of the time, Pallas kernels for 0%

profile of v1, /device:TPU:0, one launch (start us, length us, event | category | flops | bytes accessed | tf_op | source)
XLA Modules:
  0.0 969.0 jit_solution(15299070539994922334)
XLA Ops:
  9.4 1.2 gather_fusion
  10.7 2.4 gather_fusion.1
  13.5 2.4 select_multiply_fusion
  15.9 1.7 fusion.222
  19.8 99.5 %all-gather.11.cloned.1.call-done = f32[1,2,6144,128]{3,2,1,0:T(8,128)} async-done(((f32[1,2,768,128]{3,2,1,0:T(8,128)}), f32[1,2,6144,128]{3,2,1,0:T(8,128)}) %all-gather.11.cloned.1.call-update) | async-done | bytes 6291472 | tf_op jit(solution)/shard_map/all_gather | solution.py:74
  119.2 36.1 %fusion.8 = f32[128,1536]{1,0:T(8,128)S(1)} fusion(f32[2,1536,6144]{2,1,0:T(8,128)} %param.6, f32[1,2,6144,128]{3,2,1,0:T(8,128)} %all-gather.11.cloned.1.call-done), kind=kOutput, calls=%fused_computation.13 | convolution fusion | flops 14495514624 | bytes 41680896 | tf_op jit(solution)/shard_map/dot_general | solution.py:28
  155.3 35.0 %fusion.10 = f32[128,1536]{1,0:T(8,128)S(1)} fusion(f32[2,1536,6144]{2,1,0:T(8,128)} %param.6, f32[1,2,6144,128]{3,2,1,0:T(8,128)S(1)} %copy-done.2), kind=kOutput, calls=%fused_computation.15 | convolution fusion | flops 14495514624 | bytes 41680896 | tf_op jit(solution)/shard_map/dot_general | solution.py:28
  190.4 35.3 %fusion.73 = f32[1,1536,128]{1,2,0:T(8,128)S(1)} fusion(f32[128,1536]{1,0:T(8,128)S(1)} %fusion.8, f32[2,1536,6144]{2,1,0:T(8,128)} %param.6, f32[1,2,6144,128]{3,2,1,0:T(8,128)S(1)} %copy-done.2), kind=kOutput, calls=%fused_computation.79 | convolution fusion | flops 14495711232 | bytes 42467328 | tf_op jit(solution)/shard_map/dot_general | solution.py:28
  225.7 35.6 %fusion.67 = f32[1,1536,128]{1,2,0:T(8,128)S(1)} fusion(f32[128,1536]{1,0:T(8,128)S(1)} %fusion.10, f32[2,1536,6144]{2,1,0:T(8,128)} %param.6, f32[1,2,6144,128]{3,2,1,0:T(8,128)S(1)} %copy-done.2), kind=kOutput, calls=%fused_computation.77 | convolution fusion | flops 14495711232 | bytes 42467328 | tf_op jit(solution)/shard_map/dot_general | solution.py:28
  261.3 36.5 %fusion.4 = f32[128,1536]{1,0:T(8,128)S(1)} fusion(f32[2,1536,6144]{2,1,0:T(8,128)} %param.6, f32[1,2,6144,128]{3,2,1,0:T(8,128)} %all-gather.13.cloned.1.call-done), kind=kOutput, calls=%fused_computation.9 | convolution fusion | flops 14495514624 | bytes 41680896 | tf_op jit(solution)/shard_map/dot_general | solution.py:28
  297.9 35.2 %fusion.6 = f32[128,1536]{1,0:T(8,128)S(1)} fusion(f32[2,1536,6144]{2,1,0:T(8,128)} %param.6, f32[1,2,6144,128]{3,2,1,0:T(8,128)S(1)} %copy-done.3), kind=kOutput, calls=%fused_computation.11 | convolution fusion | flops 14495514624 | bytes 41680896 | tf_op jit(solution)/shard_map/dot_general | solution.py:28
  333.1 1.3 pad_maximum_fusion.3
  334.4 35.2 %fusion.85 = f32[1,1536,128]{1,2,0:T(8,128)S(1)} fusion(f32[128,1536]{1,0:T(8,128)S(1)} %fusion.4, f32[2,1536,6144]{2,1,0:T(8,128)} %param.6, f32[1,2,6144,128]{3,2,1,0:T(8,128)S(1)} %copy-done.3), kind=kOutput, calls=%fused_computation.83 | convolution fusion | flops 14495711232 | bytes 42467328 | tf_op jit(solution)/shard_map/dot_general | solution.py:28
  369.6 35.1 %fusion.79 = f32[1,1536,128]{1,2,0:T(8,128)S(1)} fusion(f32[128,1536]{1,0:T(8,128)S(1)} %fusion.6, f32[2,1536,6144]{2,1,0:T(8,128)} %param.6, f32[1,2,6144,128]{3,2,1,0:T(8,128)S(1)} %copy-done.3), kind=kOutput, calls=%fused_computation.81 | convolution fusion | flops 14495711232 | bytes 42467328 | tf_op jit(solution)/shard_map/dot_general | solution.py:28
  404.6 1.3 pad_maximum_fusion.4
  405.9 36.3 %fusion = f32[128,1536]{1,0:T(8,128)S(1)} fusion(f32[2,1536,6144]{2,1,0:T(8,128)} %param.6, f32[1,2,6144,128]{3,2,1,0:T(8,128)} %all-gather.15.cloned.1.call-done), kind=kOutput, calls=%fused_computation.5 | convolution fusion | flops 14495514624 | bytes 41680896 | tf_op jit(solution)/shard_map/dot_general | solution.py:28
  442.2 35.0 %fusion.2 = f32[128,1536]{1,0:T(8,128)S(1)} fusion(f32[2,1536,6144]{2,1,0:T(8,128)} %param.6, f32[1,2,6144,128]{3,2,1,0:T(8,128)S(1)} %copy-done.4), kind=kOutput, calls=%fused_computation.7 | convolution fusion | flops 14495514624 | bytes 41680896 | tf_op jit(solution)/shard_map/dot_general | solution.py:28
  477.3 35.5 %fusion.97 = f32[1,1536,128]{1,2,0:T(8,128)S(1)} fusion(f32[128,1536]{1,0:T(8,128)S(1)} %fusion, f32[2,1536,6144]{2,1,0:T(8,128)} %param.6, f32[1,2,6144,128]{3,2,1,0:T(8,128)S(1)} %copy-done.4), kind=kOutput, calls=%fused_computation.87 | convolution fusion | flops 14495711232 | bytes 42467328 | tf_op jit(solution)/shard_map/dot_general | solution.py:28
  512.7 35.0 %fusion.91 = f32[1,1536,128]{1,2,0:T(8,128)S(1)} fusion(f32[128,1536]{1,0:T(8,128)S(1)} %fusion.2, f32[2,1536,6144]{2,1,0:T(8,128)} %param.6, f32[1,2,6144,128]{3,2,1,0:T(8,128)S(1)} %copy-done.4), kind=kOutput, calls=%fused_computation.85 | convolution fusion | flops 14495711232 | bytes 42467328 | tf_op jit(solution)/shard_map/dot_general | solution.py:28
  547.8 1.3 pad_maximum_fusion.5
  549.0 36.3 %fusion.12 = f32[128,1536]{1,0:T(8,128)S(1)} fusion(f32[2,1536,6144]{2,1,0:T(8,128)} %param.6, f32[1,2,6144,128]{3,2,1,0:T(8,128)} %all-gather.9.cloned.1.call-done), kind=kOutput, calls=%fused_computation.17 | convolution fusion | flops 14495514624 | bytes 41680896 | tf_op jit(solution)/shard_map/dot_general | solution.py:28
  585.3 35.0 %fusion.14 = f32[128,1536]{1,0:T(8,128)S(1)} fusion(f32[2,1536,6144]{2,1,0:T(8,128)} %param.6, f32[1,2,6144,128]{3,2,1,0:T(8,128)S(1)} %copy-done.5), kind=kOutput, calls=%fused_computation.19 | convolution fusion | flops 14495514624 | bytes 41680896 | tf_op jit(solution)/shard_map/dot_general | solution.py:28
  620.4 35.5 %fusion.61 = f32[1,1536,128]{1,2,0:T(8,128)S(1)} fusion(f32[128,1536]{1,0:T(8,128)S(1)} %fusion.12, f32[2,1536,6144]{2,1,0:T(8,128)} %param.6, f32[1,2,6144,128]{3,2,1,0:T(8,128)S(1)} %copy-done.5), kind=kOutput, calls=%fused_computation.75 | convolution fusion | flops 14495711232 | bytes 42467328 | tf_op jit(solution)/shard_map/dot_general | solution.py:28
  655.9 35.0 %fusion.55 = f32[1,1536,128]{1,2,0:T(8,128)S(1)} fusion(f32[128,1536]{1,0:T(8,128)S(1)} %fusion.14, f32[2,1536,6144]{2,1,0:T(8,128)} %param.6, f32[1,2,6144,128]{3,2,1,0:T(8,128)S(1)} %copy-done.5), kind=kOutput, calls=%fused_computation.73 | convolution fusion | flops 14495711232 | bytes 42467328 | tf_op jit(solution)/shard_map/dot_general | solution.py:28
  690.9 1.3 pad_maximum_fusion.2
  692.3 1.6 dynamic-slice_multiply_fusion.2
  693.9 2.2 dynamic-slice_multiply_fusion.1
  696.1 2.3 dynamic-slice_multiply_fusion
  698.4 2.5 dynamic-slice_multiply_fusion.3
  701.0 2.9 pad_maximum_fusion.1
  704.3 1.7 gather_fusion.2
  708.4 14.6 %all-reduce.12.cloned.1.call-done = (f32[2,1536,128]{1,2,0:T(8,128)}, f32[2,1536,128]{1,2,0:T(8,128)}, f32[2,1536,128]{1,2,0:T(8,128)}, f32[2,1536,128]{1,2,0:T(8,128)}) async-done(((f32[2,1536,128]{1,2,0:T(8,128)}, f32[2,1536,128]{1,2,0:T(8,128)}, f32[2,1536,128]{1,2,0:T(8,128)}, f32[2,1536,128]{1,2,0:T(8,128)}), (f32[2,1536,128]{1,2,0:T(8,128)}, f32[2,1536,128]{1,2,0:T(8,128)}, f32[2,1536,128]{1,2,0:T(8,128)}, ...) | async-done | bytes 6291472 | tf_op jit(solution)/shard_map/psum | solution.py:76
  723.0 1.7 broadcast_multiply_fusion
  728.7 1.4 fusion.225
  730.1 1.4 fusion.224
  732.7 3.3 fusion.220
  740.3 1.1 fusion.132
  743.3 0.9 fusion.49
  744.2 0.9 fusion.48
  746.8 1.6 fusion.135
  748.4 1.4 fusion.136
  749.8 1.4 fusion.133
  751.2 1.6 fusion.134
  753.4 1.1 fusion.130
  758.6 1.8 fusion.110
  760.4 1.6 fusion.111
  762.1 1.9 fusion.106
  764.0 1.8 fusion.107
  765.8 1.8 fusion.108
  770.9 2.9 pad_maximum_fusion
  773.8 6.6 copy.33
  780.4 3.2 broadcast_in_dim.45
  783.6 13.1 %scatter_fusion = f32[4,2,1536,128]{3,2,1,0:T(8,128)} fusion(f32[4,2,1536,128]{3,2,1,0:T(8,128)} %broadcast_in_dim.45, s32[4]{0:T(128)S(1)} %copy-done.49, f32[4,2,1536,128]{3,2,1,0:T(8,128)} %copy.33), kind=kCustom, calls=%fused_computation.3 | custom fusion | bytes 18874384 | tf_op jit(solution)/shard_map/scatter | solution.py:128
  797.9 51.7 %all-reduce.6.cloned.1.call-done = f32[2,2,128,128]{3,2,1,0:T(8,128)} async-done(((f32[2,2,128,128]{3,2,1,0:T(8,128)}), f32[2,2,128,128]{3,2,1,0:T(8,128)}) %all-reduce.6.cloned.1.call-update) | async-done | bytes 262160 | tf_op jit(solution)/shard_map/psum | solution.py:112
  849.6 1.0 slice_subtract_fusion.3
  851.6 19.4 %all-reduce.8.cloned.1.call-done = f32[4,2,128,128]{3,2,1,0:T(8,128)} async-done(((f32[4,2,128,128]{3,2,1,0:T(8,128)}), f32[4,2,128,128]{3,2,1,0:T(8,128)}) %all-reduce.8.cloned.1.call-update) | async-done | bytes 524304 | tf_op jit(solution)/shard_map/psum | solution.py:10
  871.7 76.6 %all-reduce.10.cloned.1.call-done = f32[4,2,128,128]{3,2,1,0:T(8,128)} async-done(((f32[4,2,128,128]{3,2,1,0:T(8,128)}), f32[4,2,128,128]{3,2,1,0:T(8,128)}) %all-reduce.10.cloned.1.call-update) | async-done | bytes 524304 | tf_op jit(solution)/shard_map/psum | solution.py:10
  948.3 1.0 fusion.140
  950.6 1.3 fusion.104
  951.9 1.1 fusion.105
  953.0 1.1 fusion.102
  954.2 1.1 fusion.103
  955.3 1.4 fusion.142
  959.1 2.7 scatter_fusion.1
  (193 shorter events, 34.3 us)
Async XLA Ops:
  7.2 3.6 copy-start
  7.2 112.1 %all-gather.11.cloned.1.call-start = ((), (), s32[]{:S(2)}) async-start(), calls=%async_computation.4 | async-start | bytes 7077888 | tf_op jit(solution)/shard_map/all_gather | solution.py:74
  8.0 5.5 copy-start.50
  9.4 3.8 copy-start.47
  10.7 2.4 copy-start.52
  10.7 2.4 copy-start.54
  17.7 243.7 %all-gather.13.cloned.1.call-start = ((), (), s32[]{:S(2)}) async-start(), calls=%async_computation.5 | async-start | bytes 7077888 | tf_op jit(solution)/shard_map/all_gather | solution.py:74
  18.4 387.5 %all-gather.15.cloned.1.call-start = ((), (), s32[]{:S(2)}) async-start(), calls=%async_computation.6 | async-start | bytes 7077888 | tf_op jit(solution)/shard_map/all_gather | solution.py:74
  19.1 529.9 %all-gather.9.cloned.1.call-start = ((), (), s32[]{:S(2)}) async-start(), calls=%async_computation.3 | async-start | bytes 7077888 | tf_op jit(solution)/shard_map/all_gather | solution.py:74
  19.7 703.3 %all-reduce.12.cloned.1.call-start = ((), (), s32[]{:S(2)}) async-start(), calls=%async_computation.7 | async-start | bytes 12582912 | tf_op jit(solution)/shard_map/psum | solution.py:76
  119.2 36.1 %copy-start.2 = (f32[1,2,6144,128]{3,2,1,0:T(8,128)S(1)}, f32[1,2,6144,128]{3,2,1,0:T(8,128)}, u32[]{:S(2)}) copy-start(f32[1,2,6144,128]{3,2,1,0:T(8,128)} %all-gather.11.cloned.1.call-done) | copy-start | bytes 18874372
  261.3 36.6 %copy-start.3 = (f32[1,2,6144,128]{3,2,1,0:T(8,128)S(1)}, f32[1,2,6144,128]{3,2,1,0:T(8,128)}, u32[]{:S(2)}) copy-start(f32[1,2,6144,128]{3,2,1,0:T(8,128)} %all-gather.13.cloned.1.call-done) | copy-start | bytes 18874372
  405.9 36.3 %copy-start.4 = (f32[1,2,6144,128]{3,2,1,0:T(8,128)S(1)}, f32[1,2,6144,128]{3,2,1,0:T(8,128)}, u32[]{:S(2)}) copy-start(f32[1,2,6144,128]{3,2,1,0:T(8,128)} %all-gather.15.cloned.1.call-done) | copy-start | bytes 18874372
  549.0 36.3 %copy-start.5 = (f32[1,2,6144,128]{3,2,1,0:T(8,128)S(1)}, f32[1,2,6144,128]{3,2,1,0:T(8,128)}, u32[]{:S(2)}) copy-start(f32[1,2,6144,128]{3,2,1,0:T(8,128)} %all-gather.9.cloned.1.call-done) | copy-start | bytes 18874372
  692.2 157.4 %all-reduce.6.cloned.1.call-start = ((), (), s32[]{:S(2)}) async-start(), calls=%async_computation | async-start | bytes 524288 | tf_op jit(solution)/shard_map/psum | solution.py:112
  693.9 7.1 copy-start.10
  696.0 4.9 copy-start.12
  698.4 5.5 copy-start.14
  700.9 3.4 copy-start.16
  701.0 5.2 copy-start.53
  701.0 5.2 copy-start.55
  701.0 5.8 copy-start.27
  701.0 6.5 copy-start.51
  704.3 27.2 %collective-permute-start = (f32[4,2,1536,128]{3,2,1,0:T(8,128)}, f32[4,2,1536,128]{3,2,1,0:T(8,128)}, u32[]{:S(2)}, u32[]{:S(2)}) collective-permute-start(f32[4,2,1536,128]{3,2,1,0:T(8,128)} %pad_maximum_fusion.1), channel_id=1, source_target_pairs={{0,1},{1,0},{2,3},{3,2},{4,5},{5,4},{6,7},{7,6},{8,9},{9,8},{10,11... | collective-permute-start | bytes 18874376 | tf_op jit(solution)/shard_map/ppermute | solution.py:24
  723.0 1.9 copy-start.30
  725.2 15.1 %copy-start.23 = (f32[2,128,768]{2,1,0:T(8,128)}, f32[2,128,768]{2,1,0:T(8,128)S(1)}, u32[]{:S(2)}) copy-start(f32[2,128,768]{2,1,0:T(8,128)S(1)} %get-tuple-element.39) | copy-start | bytes 2359300
  725.2 28.1 %copy-start.21 = (f32[2,128,768]{2,1,0:T(8,128)}, f32[2,128,768]{2,1,0:T(8,128)S(1)}, u32[]{:S(2)}) copy-start(f32[2,128,768]{2,1,0:T(8,128)S(1)} %get-tuple-element.40) | copy-start | bytes 2359300
  725.2 3.4 copy-start.31
  728.7 2.8 copy-start.11
  728.7 2.8 copy-start.13
  728.7 3.5 copy-start.15
  728.7 3.9 copy-start.17
  736.4 8.7 copy-start.20
  736.4 16.9 %copy-start.18 = (f32[1,2,1536,128]{3,2,1,0:T(8,128)}, f32[1,2,1536,128]{3,2,1,0:T(8,128)S(1)}, u32[]{:S(2)}) copy-start(f32[1,2,1536,128]{3,2,1,0:T(8,128)S(1)} %get-tuple-element.13) | copy-start | bytes 4718596
  744.2 1.4 copy-start.35
  744.2 1.9 copy-start.36
  745.3 3.1 copy-start.26
  745.3 6.0 copy-start.24
  746.7 9.4 copy-start.6
  746.8 9.4 copy-start.8
  756.9 8.9 copy-start.7
  757.7 4.3 copy-start.9
  758.5 112.5 %all-reduce.8.cloned.1.call-start = ((), (), s32[]{:S(2)}) async-start(), calls=%async_computation.1 | async-start | bytes 1048576 | tf_op jit(solution)/shard_map/psum | solution.py:10
  758.6 9.1 copy-start.25
  758.6 9.1 copy-start.45
  758.6 9.9 %copy-start.19 = (f32[1,2,1536,128]{3,2,1,0:T(8,128)S(1)}, f32[1,2,1536,128]{3,2,1,0:T(8,128)}, u32[]{:S(2)}) copy-start(f32[1,2,1536,128]{3,2,1,0:T(8,128)} %copy-done.18) | copy-start | bytes 4718596
  758.6 9.9 %copy-start.22 = (f32[2,128,768]{2,1,0:T(8,128)S(1)}, f32[2,128,768]{2,1,0:T(8,128)}, u32[]{:S(2)}) copy-start(f32[2,128,768]{2,1,0:T(8,128)} %copy-done.21) | copy-start | bytes 2359300
  758.6 10.4 %copy-start.46 = (f32[128,128]{1,0:T(8,128)S(1)}, f32[128,128]{1,0:T(8,128)}, u32[]{:S(2)}) copy-start(f32[128,128]{1,0:T(8,128)} %fusion.130) | copy-start | bytes 196612
  762.1 8.8 copy-start.28
  762.1 8.8 copy-start.29
  780.4 3.2 copy-start.49
  783.6 13.1 %copy-start.43 = (f32[1,2,128,128]{3,2,1,0:T(8,128)S(1)}, f32[1,2,128,128]{3,2,1,0:T(8,128)}, u32[]{:S(2)}) copy-start(f32[1,2,128,128]{3,2,1,0:T(8,128)} %maximum_bitcast_fusion.5) | copy-start | bytes 393220
  783.6 13.1 %copy-start.44 = (f32[1,2,128,128]{3,2,1,0:T(8,128)S(1)}, f32[1,2,128,128]{3,2,1,0:T(8,128)}, u32[]{:S(2)}) copy-start(f32[1,2,128,128]{3,2,1,0:T(8,128)} %maximum_bitcast_fusion.4) | copy-start | bytes 393220
  783.6 65.9 %copy-start.32 = (f32[4,2,128,128]{3,2,1,0:T(8,128)S(1)}, f32[4,2,128,128]{3,2,1,0:T(8,128)}, u32[]{:S(2)}) copy-start(f32[4,2,128,128]{3,2,1,0:T(8,128)} %broadcast_select_fusion) | copy-start | bytes 1572868
  796.7 152.7 %copy-start.38 = (f32[2,128,128]{1,2,0:T(8,128)S(1)}, f32[2,128,128]{1,2,0:T(8,128)}, u32[]{:S(2)}) copy-start(f32[2,128,128]{1,2,0:T(8,128)} %get-tuple-element.29) | copy-start | bytes 393220
  796.7 153.3 %copy-start.37 = (f32[2,128,128]{1,2,0:T(8,128)S(1)}, f32[2,128,128]{1,2,0:T(8,128)}, u32[]{:S(2)}) copy-start(f32[2,128,128]{1,2,0:T(8,128)} %get-tuple-element.30) | copy-start | bytes 393220
  797.6 150.8 %all-reduce.10.cloned.1.call-start = ((), (), s32[]{:S(2)}) async-start(), calls=%async_computation.2 | async-start | bytes 1048576 | tf_op jit(solution)/shard_map/psum | solution.py:10
  850.6 21.1 %copy-start.33 = (f32[1,2,128,128]{3,2,1,0:T(8,128)}, f32[1,2,128,128]{3,2,1,0:T(8,128)S(1)}, u32[]{:S(2)}) copy-start(f32[1,2,128,128]{3,2,1,0:T(8,128)S(1)} %get-tuple-element.22) | copy-start | bytes 393220
  851.4 98.6 %copy-start.39 = (f32[128,128]{1,0:T(8,128)}, f32[128,128]{1,0:T(8,128)S(1)}, u32[]{:S(2)}) copy-start(f32[128,128]{1,0:T(8,128)S(1)} %convolution_add_fusion.5) | copy-start | bytes 196612
  851.6 98.3 %copy-start.40 = (f32[128,128]{1,0:T(8,128)}, f32[128,128]{1,0:T(8,128)S(1)}, u32[]{:S(2)}) copy-start(f32[128,128]{1,0:T(8,128)S(1)} %convolution_subtract_fusion.5) | copy-start | bytes 196612
  871.5 78.5 %copy-start.41 = (f32[128,128]{1,0:T(8,128)}, f32[128,128]{1,0:T(8,128)S(1)}, u32[]{:S(2)}) copy-start(f32[128,128]{1,0:T(8,128)S(1)} %convolution_add_fusion.3) | copy-start | bytes 196612
  871.7 78.6 %copy-start.42 = (f32[128,128]{1,0:T(8,128)}, f32[128,128]{1,0:T(8,128)S(1)}, u32[]{:S(2)}) copy-start(f32[128,128]{1,0:T(8,128)S(1)} %convolution_subtract_fusion.3) | copy-start | bytes 196612
  948.3 9.1 copy-start.34
  950.6 11.2 %copy-start.1 = (f32[4,2,768,128]{3,2,1,0:T(8,128)S(1)}, f32[4,2,768,128]{3,2,1,0:T(8,128)}, u32[]{:S(2)}) copy-start(f32[4,2,768,128]{3,2,1,0:T(8,128)} %param.7) | copy-start | bytes 9437188
  (1 other events, 0.6 us)
Sparse Core Ops, SparseCore 0:
  17.8 101.4 all-gather.10
  121.4 96.8 all-gather.12
  220.5 96.9 all-gather.14
  320.1 96.8 all-gather.8
  692.3 30.6 all-reduce.11
  758.7 90.8 all-reduce.5
  851.9 19.0 all-reduce.7
  874.4 73.8 all-reduce.9
